TPU v7x, 32 devices: a whole 2x2x4 slice. The times are simulated.
32 devices in a mesh: frame: 8 (over y, x, core), head: 4 (over z).
Axes of the slice: x: 2, y: 2, z: 4, core: 2. Of those that a mesh axis runs over, the one named last changes fastest.
Arguments:
- queries: bfloat16 [4, 2048, 4096], P(None, 'frame', 'head'), may hold values from -6 to 6
- keys: bfloat16 [4, 2048, 4096], P(None, 'frame', 'head'), may hold values from -6 to 6
- values: bfloat16 [4, 2048, 4096], P(None, 'frame', 'head'), may hold values from -6 to 6
- step_sizes: bfloat16 [4, 2048, 16], P(None, 'frame', 'head'), may hold values from 9e-05 to 1.25, as said below
- starts: int32 [4], replicated, may hold values from 0 to 7, as said below
- resets: int32 [4, 8], replicated, may hold values 0 or 1
- init_in: bfloat16 [16, 256, 1024], P('head'), may hold values from -0.375 to 0.375
- init_out: bfloat16 [16, 512, 256], P('head'), may hold values from -0.25 to 0.25
- gain: float32 [4096], P('head'), may hold values from 0.25 to 1.75
- out_proj: bfloat16 [4096, 5120], P('head'), may hold values from -0.125 to 0.125
Outputs:
- mixed_out: bfloat16 [4, 2048, 5120], P(None, 'frame', 'head')
Inputs may be any that keep to these rules, and one draw needn't show every extreme that they name: `starts`: 4 distinct blocks. `step_sizes`: positive.
All inputs are finite; a program needn't handle non-finite values.
Results may differ from a plain program's by a relative error of at most 0.035.
Values may be sent and summed in bfloat16 or wider, within the bound.
No kernel may reach another device: no remote copies, remote signals or barrier semaphores. Data moves between devices by JAX's collectives and lax.ppermute only.
A program may use at most 128 MiB of HBM per device.

v0:
```python
import jax
import jax.numpy as jnp
from jax import lax
from jax.sharding import PartitionSpec as P


def renorm(raw_weights, target):
    column_scale = target[:, None, :] * lax.rsqrt(
        jnp.sum(raw_weights * raw_weights, axis=1, keepdims=True) + 1e-06
    )
    return (raw_weights * column_scale).astype(jnp.bfloat16)


def advance(
    weights_in, weights_out, queries_seg, keys_seg, values_seg, rates_seg, norm_in, norm_out, gain
):
    rows_here = queries_seg.shape[0]
    heads_here = weights_in.shape[0]
    head_width = weights_in.shape[1]
    hidden_width = weights_out.shape[1]
    key_heads = keys_seg.reshape(rows_here, heads_here, head_width)
    pre_keys = jnp.einsum("thd,hde->hte", key_heads, weights_in, preferred_element_type=jnp.float32)
    first_half = pre_keys[..., :hidden_width]
    second_half = pre_keys[..., hidden_width:]
    sigmoid_first = jax.nn.sigmoid(first_half)
    activated = first_half * sigmoid_first
    hidden = (activated * second_half).astype(jnp.bfloat16)
    value_heads = values_seg.reshape(rows_here, heads_here, head_width).astype(jnp.float32)
    scaled = (value_heads * rates_seg.astype(jnp.float32)[:, :, None]).astype(jnp.bfloat16)
    grad_hidden = jnp.einsum(
        "the,hfe->htf", scaled, weights_out, preferred_element_type=jnp.float32
    )
    grad_first = (
        grad_hidden * second_half * sigmoid_first * (1.0 + first_half * (1.0 - sigmoid_first))
    )
    grad_second = grad_hidden * activated
    grad_pre = jnp.concatenate([grad_first, grad_second], axis=-1).astype(jnp.bfloat16)
    raw_in = weights_in.astype(jnp.float32) + jnp.einsum(
        "thd,hte->hde", key_heads, grad_pre, preferred_element_type=jnp.float32
    )
    raw_out = weights_out.astype(jnp.float32) + jnp.einsum(
        "htf,the->hfe", hidden, scaled, preferred_element_type=jnp.float32
    )
    new_in = renorm(raw_in, norm_in)
    new_out = renorm(raw_out, norm_out)
    query_heads = queries_seg.reshape(rows_here, heads_here, head_width)
    pre_queries = jnp.einsum(
        "thd,hde->hte", query_heads, new_in, preferred_element_type=jnp.float32
    )
    hidden_queries = (
        jax.nn.silu(pre_queries[..., :hidden_width]) * pre_queries[..., hidden_width:]
    ).astype(jnp.bfloat16)
    fast_out = jnp.einsum(
        "htf,hfe->the", hidden_queries, new_out, preferred_element_type=jnp.float32
    )
    normed = fast_out * lax.rsqrt(jnp.mean(fast_out * fast_out, axis=-1, keepdims=True) + 1e-05)
    normed = normed * gain.reshape(heads_here, head_width)
    return (
        new_in,
        new_out,
        normed.reshape(rows_here, heads_here * head_width).astype(jnp.bfloat16),
    )


def shards(queries, keys, values, step_sizes, starts, resets, init_in, init_out, gain, out_proj):
    frames = lax.axis_size("frame")
    position = lax.axis_index("frame")
    videos = queries.shape[0]
    rows_block = queries.shape[1]
    norm_in = jnp.sqrt(jnp.sum(jnp.square(init_in.astype(jnp.float32)), axis=1))
    norm_out = jnp.sqrt(jnp.sum(jnp.square(init_out.astype(jnp.float32)), axis=1))
    padding = ((0, frames - videos), (0, 0), (0, 0))
    moved_queries, moved_keys, moved_values, moved_rates = (
        lax.all_to_all(jnp.pad(queries, padding), "frame", split_axis=0, concat_axis=1, tiled=True),
        lax.all_to_all(jnp.pad(keys, padding), "frame", split_axis=0, concat_axis=1, tiled=True),
        lax.all_to_all(jnp.pad(values, padding), "frame", split_axis=0, concat_axis=1, tiled=True),
        lax.all_to_all(
            jnp.pad(step_sizes, padding), "frame", split_axis=0, concat_axis=1, tiled=True
        ),
    )
    video_here = jnp.minimum(position, videos - 1)
    first_block = starts[video_here]
    reset_flags = resets[video_here]

    def local_segment(seg_index, loop_state):
        state_in, state_out, collected = loop_state
        block_now = (first_block + seg_index) % frames
        first_row = block_now * rows_block
        queries_seg = lax.dynamic_slice_in_dim(moved_queries[0], first_row, rows_block, 0)
        keys_seg = lax.dynamic_slice_in_dim(moved_keys[0], first_row, rows_block, 0)
        values_seg = lax.dynamic_slice_in_dim(moved_values[0], first_row, rows_block, 0)
        rates_seg = lax.dynamic_slice_in_dim(moved_rates[0], first_row, rows_block, 0)
        restart = jnp.logical_or(seg_index == 0, reset_flags[seg_index] == 1)
        weights_in = jnp.where(restart, init_in, state_in)
        weights_out = jnp.where(restart, init_out, state_out)
        new_in, new_out, normed = advance(
            weights_in,
            weights_out,
            queries_seg,
            keys_seg,
            values_seg,
            rates_seg,
            norm_in,
            norm_out,
            gain,
        )
        collected = lax.dynamic_update_slice_in_dim(collected, normed, first_row, 0)
        return (new_in, new_out, collected)

    empty_rows = jnp.zeros((moved_queries.shape[1], moved_queries.shape[2]), jnp.bfloat16)
    _, _, own_rows = lax.fori_loop(0, frames, local_segment, (init_in, init_out, empty_rows))
    returned = lax.all_to_all(own_rows[None], "frame", split_axis=1, concat_axis=0, tiled=True)
    normed_all = returned[:videos]
    flat_rows = normed_all.reshape(videos * rows_block, normed_all.shape[2])
    partial_value = jnp.dot(flat_rows, out_proj, preferred_element_type=jnp.float32)
    mixed_out = lax.psum_scatter(
        partial_value.astype(jnp.bfloat16), "head", scatter_dimension=1, tiled=True
    ).astype(jnp.float32)
    return mixed_out.astype(jnp.bfloat16).reshape(videos, rows_block, mixed_out.shape[1])


def solution(mesh):
    return jax.shard_map(
        shards,
        mesh=mesh,
        in_specs=(
            P(None, "frame", "head"),
            P(None, "frame", "head"),
            P(None, "frame", "head"),
            P(None, "frame", "head"),
            P(),
            P(),
            P("head", None, None),
            P("head", None, None),
            P("head"),
            P("head", None),
        ),
        out_specs=P(None, "frame", "head"),
        check_vma=False,
    )
```

profile of v0, /device:TPU:0, one launch (start us, length us, event | category | flops | bytes accessed | tf_op | source)
XLA Modules:
  0.0 665.5 jit_solution(5543504575499884247)
XLA Ops:
  7.9 5.2 all-to-all-start.2
  13.1 4.1 pad.17
  17.8 4.6 all-to-all-start.3
  22.4 2.5 pad.14
  24.9 46.6 %all-to-all-done.3 = bf16[8,256,1024]{2,1,0:T(8,128)(2,1)} async-done(((bf16[8,256,1024]{2,1,0:T(8,128)(2,1)}), bf16[8,256,1024]{2,1,0:T(8,128)(2,1)}, u32[]{:S(2)}, u32[]{:S(2)}) %all-to-all-start.3) | async-done | bytes 4194336 | tf_op jit(solution)/shard_map/all_to_all | solution.py:74
  71.5 4.6 all-to-all-start
  76.1 2.4 pad.15
  78.5 46.7 %all-to-all-done = bf16[8,256,1024]{2,1,0:T(8,128)(2,1)} async-done(((bf16[8,256,1024]{2,1,0:T(8,128)(2,1)}), bf16[8,256,1024]{2,1,0:T(8,128)(2,1)}, u32[]{:S(2)}, u32[]{:S(2)}) %all-to-all-start) | async-done | bytes 4194336 | tf_op jit(solution)/shard_map/all_to_all | solution.py:75
  125.1 4.6 all-to-all-start.1
  131.1 1.7 copy.77
  134.6 44.3 %all-to-all-done.1 = bf16[8,256,1024]{2,1,0:T(8,128)(2,1)} async-done(((bf16[8,256,1024]{2,1,0:T(8,128)(2,1)}), bf16[8,256,1024]{2,1,0:T(8,128)(2,1)}, u32[]{:S(2)}, u32[]{:S(2)}) %all-to-all-start.1) | async-done | bytes 4194336 | tf_op jit(solution)/shard_map/all_to_all | solution.py:76
  178.8 2.5 broadcast_in_dim.24
  181.3 158.4 %while.20 = (s32[]{:T(128)}, bf16[4,256,1024]{2,1,0:T(8,128)(2,1)S(1)}, bf16[4,512,256]{2,1,0:T(8,128)(2,1)}, bf16[2048,1024]{0,1:T(8,128)(2,1)}, s32[8]{0:T(128...) while((s32[]{:T(128)}, ...), condition=%wide.wide.region_6.7_spmd, body=%wide.wide.region_2.6_spmd.sunk | while | flops 2449480704 | bytes 95033920 | solution.py:111
  184.5 2.4 dynamic-slice_convert_fusion.3
  186.9 2.7 reshape.137
  190.6 1.9 broadcast_select_fusion.5
  194.4 1.6 multiply_convert_fusion.15
  205.7 2.4 dynamic-slice_convert_fusion.3
  208.1 2.7 reshape.137
  214.0 1.5 multiply_convert_fusion.15
  215.5 1.4 multiply_reduce_fusion.12
  225.3 2.4 dynamic-slice_convert_fusion.3
  227.7 2.7 reshape.137
  233.6 1.6 multiply_convert_fusion.15
  244.9 2.4 dynamic-slice_convert_fusion.3
  247.3 2.7 reshape.137
  253.2 1.6 multiply_convert_fusion.15
  254.7 1.4 multiply_reduce_fusion.12
  264.5 2.4 dynamic-slice_convert_fusion.3
  266.9 2.7 reshape.137
  272.7 1.6 multiply_convert_fusion.15
  284.1 2.4 dynamic-slice_convert_fusion.3
  286.5 2.7 reshape.137
  292.3 1.6 multiply_convert_fusion.15
  303.7 2.4 dynamic-slice_convert_fusion.3
  306.1 2.7 reshape.137
  312.0 1.5 multiply_convert_fusion.15
  323.3 2.4 dynamic-slice_convert_fusion.3
  325.7 2.7 reshape.137
  331.6 1.6 multiply_convert_fusion.15
  339.7 20.5 %copy.42 = bf16[1,2048,1024]{2,0,1:T(2,128)(2,1)} copy(bf16[1,2048,1024]{1,2,0:T(8,128)(2,1)} %bitcast.69) | data formatting | bytes 8388608 | tf_op jit(solution)/shard_map/broadcast_in_dim | solution.py:112
  360.7 26.0 %reduce = bf16[2048,1024]{1,0:T(8,128)(2,1)} reduce(bf16[2048,1,1024]{2,1,0:T(2,128)(2,1)} %bitcast.67, bf16[]{:T(256)} %broadcast.99), dimensions={1}, to_apply=%bitcast.20.reduce_sub_computation | reduce | bytes 8388610
  386.7 7.8 %reshape.133 = bf16[8,2,131072]{2,1,0:T(2,128)(2,1)} reshape(bf16[2048,1024]{1,0:T(8,128)(2,1)} %reduce) | data formatting | bytes 8388608
  394.5 54.2 %all_to_all.60 = bf16[8,2,131072]{2,1,0:T(2,128)(2,1)} all-to-all(bf16[8,2,131072]{2,1,0:T(2,128)(2,1)} %reshape.133), channel_id=1, replica_groups=mesh['frame'=8,'head'=4] {'frame'}, dimensions={0} | all-to-all | bytes 8388608 | tf_op jit(solution)/shard_map/all_to_all | solution.py:112
  448.7 8.8 %reshape.134 = bf16[2048,1,1024]{2,1,0:T(2,128)(2,1)} reshape(bf16[8,2,131072]{2,1,0:T(2,128)(2,1)} %all_to_all.60) | data formatting | bytes 8388608
  457.4 5.1 copy.53
  462.7 17.2 %convolution_convert_fusion = bf16[1024,5120]{1,0:T(8,128)(2,1)} fusion(bf16[1024,1024]{1,0:T(8,128)(2,1)S(1)} %bitcast.71, bf16[1024,5120]{1,0:T(8,128)(2,1)} %param.21), kind=kOutput, calls=%fused_computation.36 | convolution fusion | flops 10742661120 | bytes 23068672 | tf_op jit(solution)/shard_map/dot_general | solution.py:115
  480.0 178.6 %reduce-scatter.2.cloned.1.call-done = bf16[1024,1280]{1,0:T(8,128)(2,1)} async-done(((bf16[1024,5120]{1,0:T(8,128)(2,1)}), bf16[1024,1280]{1,0:T(8,128)(2,1)}) %reduce-scatter.2.cloned.1.call-update) | async-done | bytes 2621456 | tf_op jit(solution)/shard_map/reduce_scatter | solution.py:116
  (251 shorter events, 94.9 us)
Async XLA Ops:
  6.5 128.0 %copy-start = (s32[4,8]{1,0:T(4,128)S(1)}, s32[4,8]{1,0:T(4,128)}, u32[]{:S(2)}) copy-start(s32[4,8]{1,0:T(4,128)} %param.17) | copy-start | bytes 388
  7.9 10.0 %all-to-all-start.2 = ((bf16[8,256,4]{1,2,0:T(4,128)(2,1)}), bf16[8,256,4]{1,2,0:T(4,128)(2,1)S(1)}, u32[]{:S(2)}, u32[]{:S(2)}) async-start(bf16[8,256,4]{1,2,0:T(4,128)(2,1)} %pad.16), calls=%async_computation.2 | async-start | bytes 32768 | tf_op jit(solution)/shard_map/all_to_all | solution.py:77
  17.1 5.3 copy-start.7
  17.8 53.7 %all-to-all-start.3 = ((bf16[8,256,1024]{2,1,0:T(8,128)(2,1)}), bf16[8,256,1024]{2,1,0:T(8,128)(2,1)}, u32[]{:S(2)}, u32[]{:S(2)}) async-start(bf16[8,256,1024]{2,1,0:T(8,128)(2,1)} %pad.17), calls=%async_computation.3 | async-start | bytes 8388608 | tf_op jit(solution)/shard_map/all_to_all | solution.py:74
  24.9 51.2 %copy-start.8 = (bf16[4,256,1024]{2,1,0:T(8,128)(2,1)S(1)}, bf16[4,256,1024]{2,1,0:T(8,128)(2,1)}, u32[]{:S(2)}) copy-start(bf16[4,256,1024]{2,1,0:T(8,128)(2,1)} %param.14) | copy-start | bytes 6291460
  71.5 53.7 %all-to-all-start = ((bf16[8,256,1024]{2,1,0:T(8,128)(2,1)}), bf16[8,256,1024]{2,1,0:T(8,128)(2,1)}, u32[]{:S(2)}, u32[]{:S(2)}) async-start(bf16[8,256,1024]{2,1,0:T(8,128)(2,1)} %pad.14), calls=%async_computation | async-start | bytes 8388608 | tf_op jit(solution)/shard_map/all_to_all | solution.py:75
  78.5 51.3 %copy-start.11 = (f32[1024]{0:T(1024)S(1)}, f32[1024]{0:T(1024)}, u32[]{:S(2)}) copy-start(f32[1024]{0:T(1024)} %param.20) | copy-start | bytes 12292
  78.5 51.3 %copy-start.5 = (bf16[4,512,256]{2,1,0:T(8,128)(2,1)S(1)}, bf16[4,512,256]{2,1,0:T(8,128)(2,1)}, u32[]{:S(2)}) copy-start(bf16[4,512,256]{2,1,0:T(8,128)(2,1)} %param.19) | copy-start | bytes 3145732
  125.1 53.7 %all-to-all-start.1 = ((bf16[8,256,1024]{2,1,0:T(8,128)(2,1)}), bf16[8,256,1024]{2,1,0:T(8,128)(2,1)}, u32[]{:S(2)}, u32[]{:S(2)}) async-start(bf16[8,256,1024]{2,1,0:T(8,128)(2,1)} %pad.15), calls=%async_computation.1 | async-start | bytes 8388608 | tf_op jit(solution)/shard_map/all_to_all | solution.py:76
  129.7 528.9 %reduce-scatter.2.cloned.1.call-start = ((), (), s32[]{:S(2)}) async-start(), calls=%async_computation.6 | async-start | bytes 13107200 | tf_op jit(solution)/shard_map/reduce_scatter | solution.py:116
  131.0 2.2 copy-start.2
  192.5 1.2 copy-start.4
  192.5 1.5 copy-start.6
  192.5 1.8 copy-start.9
  197.6 2.8 copy-start.10
  198.6 1.0 copy-start.3
  212.1 1.2 copy-start.4
  212.1 1.5 copy-start.6
  212.1 1.8 copy-start.9
  217.2 2.8 copy-start.10
  218.2 1.0 copy-start.3
  231.7 1.2 copy-start.4
  231.7 1.5 copy-start.6
  231.8 1.8 copy-start.9
  236.8 2.8 copy-start.10
  237.8 1.0 copy-start.3
  251.3 1.2 copy-start.4
  251.3 1.5 copy-start.6
  251.3 1.8 copy-start.9
  256.4 2.8 copy-start.10
  257.4 1.0 copy-start.3
  270.9 1.2 copy-start.4
  270.9 1.5 copy-start.6
  270.9 1.8 copy-start.9
  275.9 2.8 copy-start.10
  290.5 1.2 copy-start.4
  290.5 1.5 copy-start.6
  290.5 1.8 copy-start.9
  295.5 2.8 copy-start.10
  310.1 1.2 copy-start.4
  310.1 1.5 copy-start.6
  310.1 1.8 copy-start.9
  315.2 2.8 copy-start.10
  329.7 1.2 copy-start.4
  329.7 1.5 copy-start.6
  329.7 1.8 copy-start.9
  334.8 2.8 copy-start.10
  480.0 178.6 %copy-start.1 = (s32[4,8]{1,0:T(4,128)S(1)}, s32[4,8]{1,0:T(4,128)}, u32[]{:S(2)}) copy-start(s32[4,8]{1,0:T(4,128)} %param.17) | copy-start | bytes 388
  (5 other events, 4.8 us)
Sparse Core Ops, SparseCore 0:
  480.1 178.4 reduce-scatter.1
where the time goes:
time: 669 us; the launch traced here: 665 us
  waiting for transfers between devices  317 us (47%)
  local copies, waits for them, and re-layouts  122 us (18%)
  matrix products  68.7 us (10%)
  other arithmetic  59.4 us (9%)
  blocking collectives  54.2 us (8%)
  starting transfers between devices  19 us (3%)
  between operations  13.5 us (2%)
  loops' own time  11.9 us (2%)
    reduce_scatter x1, waiting for transfers between devices, shards(): lax.psum_scatter(partial_value.astype(jnp.bfloat16), 'head', scatter_dime...  179 us
    all_to_all x1, blocking collectives, shards(): lax.all_to_all(own_rows[None], 'frame', split_axis=1, concat_axis=0, tile...  54.2 us
    all_to_all x1, waiting for transfers between devices, shards(): lax.all_to_all(jnp.pad(keys, padding), 'frame', split_axis=0, concat_axis...  46.7 us
    all_to_all x1, waiting for transfers between devices, shards(): lax.all_to_all(jnp.pad(queries, padding), 'frame', split_axis=0, concat_a...  46.6 us
    all_to_all x1, waiting for transfers between devices, shards(): lax.all_to_all(jnp.pad(values, padding), 'frame', split_axis=0, concat_ax...  44.3 us
    unnamed x1, other arithmetic  26 us
    unnamed x22, local copies, waits for them, and re-layouts  25.5 us
    convert_element_type x8, local copies, waits for them, and re-layouts, advance(): values_seg.reshape(rows_here, heads_here, head_width).astype(jnp.float32)  21.3 us
  transfers between devices with their start and end apart: 5, of which 5 were waited for; matrix products, arithmetic and copies ran while one was open for 2% of the time, Pallas kernels for 0%

commit v1 on v0

--- a/solution.py
+++ b/solution.py
@@ -2,6 +2,7 @@
 import jax.numpy as jnp
 from jax import lax
 from jax.sharding import PartitionSpec as P
+from jax.lax import all_to_all, axis_size
 
 
 def renorm(raw_weights, target):
@@ -63,6 +64,14 @@
 
 
 def shards(queries, keys, values, step_sizes, starts, resets, init_in, init_out, gain, out_proj):
+
+    def expand_cells(page, lane_axis):
+        carry_out = axis_size(lane_axis)
+        kept_arr = jnp.split(page, carry_out, axis=0)
+        moved = jnp.stack(kept_arr, axis=0)
+        upper = all_to_all(moved, axis_name=lane_axis, split_axis=0, concat_axis=0)
+        return jnp.concatenate(upper, 1)
+
     frames = lax.axis_size("frame")
     position = lax.axis_index("frame")
     videos = queries.shape[0]
@@ -72,7 +81,7 @@
     padding = ((0, frames - videos), (0, 0), (0, 0))
     moved_queries, moved_keys, moved_values, moved_rates = (
         lax.all_to_all(jnp.pad(queries, padding), "frame", split_axis=0, concat_axis=1, tiled=True),
-        lax.all_to_all(jnp.pad(keys, padding), "frame", split_axis=0, concat_axis=1, tiled=True),
+        expand_cells(jnp.pad(keys, padding), "frame"),
         lax.all_to_all(jnp.pad(values, padding), "frame", split_axis=0, concat_axis=1, tiled=True),
         lax.all_to_all(
             jnp.pad(step_sizes, padding), "frame", split_axis=0, concat_axis=1, tiled=True

time: 669 us -> 672 us (level)
  local copies, waits for them, and re-layouts: 122 us -> 139 us
  waiting for transfers between devices: 317 us -> 305 us
    while x80 -> x89, local copies, waits for them, and re-layouts: 10.6 us -> 41.2 us
    convert_element_type x8, local copies, waits for them, and re-layouts: 21.3 us -> 11.5 us  [advance(): values_seg.reshape(rows_here, heads_here, head_width).astype(jnp.float32)]
    dynamic_slice x16 -> x8, local copies, waits for them, and re-layouts: 10.3 us -> 0.63 us  [local_segment(): keys_seg = lax.dynamic_slice_in_dim(moved_keys[0], first_row, rows_block, 0)]
    all_to_all x1, waiting for transfers between devices: 44.3 us -> 37.5 us  [shards(): lax.all_to_all(jnp.pad(values, padding), 'frame', split_axis=0, concat_ax...]
    unnamed x22 -> x29, local copies, waits for them, and re-layouts: 25.5 us -> 31.1 us
  transfers between devices with their start and end apart: 5 -> 5, of which waited for: 5 -> 5; matrix products, arithmetic and copies ran while one was open for 2% -> 4% of each run, Pallas kernels for 0% -> 0%
where the time goes in v1:
time: 672 us; the launch traced here: 669 us
  waiting for transfers between devices  305 us (45%)
  local copies, waits for them, and re-layouts  139 us (21%)
  matrix products  68.7 us (10%)
  other arithmetic  58.9 us (9%)
  blocking collectives  53.6 us (8%)
  starting transfers between devices  18.9 us (3%)
  between operations  13.5 us (2%)
  loops' own time  11.9 us (2%)
    reduce_scatter x1, waiting for transfers between devices, shards(): lax.psum_scatter(partial_value.astype(jnp.bfloat16), 'head', scatter_dime...  178 us
    all_to_all x1, blocking collectives, shards(): lax.all_to_all(own_rows[None], 'frame', split_axis=1, concat_axis=0, tile...  53.6 us
    all_to_all x1, waiting for transfers between devices, expand_cells(): upper = all_to_all(moved, axis_name=lane_axis, split_axis=0, concat_axis=0)  46.6 us
    all_to_all x1, waiting for transfers between devices, shards(): lax.all_to_all(jnp.pad(queries, padding), 'frame', split_axis=0, concat_a...  42.3 us
    all_to_all x1, waiting for transfers between devices, shards(): lax.all_to_all(jnp.pad(values, padding), 'frame', split_axis=0, concat_ax...  37.5 us
    while x88, local copies, waits for them, and re-layouts  34 us
    unnamed x29, local copies, waits for them, and re-layouts  31.1 us
    unnamed x1, other arithmetic  26 us
  transfers between devices with their start and end apart: 5, of which 5 were waited for; matrix products, arithmetic and copies ran while one was open for 4% of the time, Pallas kernels for 0%

profile of v1, /device:TPU:0, one launch (start us, length us, event | category | flops | bytes accessed | tf_op | source)
XLA Modules:
  0.0 668.9 jit_solution(2173781453467331539)
XLA Ops:
  7.9 5.2 all-to-all-start.2
  13.1 4.1 pad.14
  17.8 4.6 all-to-all-start.3
  29.2 42.3 %all-to-all-done.3 = bf16[8,256,1024]{2,1,0:T(8,128)(2,1)} async-done(((bf16[8,256,1024]{2,1,0:T(8,128)(2,1)}), bf16[8,256,1024]{2,1,0:T(8,128)(2,1)}, u32[]{:S(2)}, u32[]{:S(2)}) %all-to-all-start.3) | async-done | bytes 4194336 | tf_op jit(solution)/shard_map/all_to_all | solution.py:83
  71.5 4.6 all-to-all-start
  76.1 2.4 pad.12
  78.5 46.6 %all-to-all-done = bf16[8,1,256,1024]{3,2,1,0:T(8,128)(2,1)} async-done(((bf16[8,1,256,1024]{3,2,1,0:T(8,128)(2,1)}), bf16[8,1,256,1024]{3,2,1,0:T(8,128)(2,1)}, u32[]{:S(2)}, u32[]{:S(2)}) %all-to-all-start) | async-done | bytes 4194336 | tf_op jit(solution)/shard_map/all_to_all | solution.py:72
  125.1 4.6 all-to-all-start.1
  131.0 1.7 copy.94
  134.2 7.2 %copy.51 = bf16[8,1,256,1024]{2,0,3,1:T(8,128)(2,1)} copy(bf16[8,1,256,1024]{3,2,1,0:T(8,128)(2,1)} %all-to-all-done) | data formatting | bytes 8388608 | tf_op jit(solution)/shard_map/while | solution.py:120
  141.4 37.5 %all-to-all-done.1 = bf16[8,256,1024]{2,1,0:T(8,128)(2,1)} async-done(((bf16[8,256,1024]{2,1,0:T(8,128)(2,1)}), bf16[8,256,1024]{2,1,0:T(8,128)(2,1)}, u32[]{:S(2)}, u32[]{:S(2)}) %all-to-all-start.1) | async-done | bytes 4194336 | tf_op jit(solution)/shard_map/all_to_all | solution.py:85
  178.8 2.5 broadcast_in_dim.24
  181.3 163.6 %while.20 = (s32[]{:T(128)}, bf16[4,256,1024]{2,1,0:T(8,128)(2,1)S(1)}, bf16[4,512,256]{2,1,0:T(8,128)(2,1)}, bf16[2048,1024]{0,1:T(8,128)(2,1)}, s32[8]{0:T(128...) while((s32[]{:T(128)}, ...), condition=%wide.wide.region_6.7_spmd, body=%wide.wide.region_2.6_spmd.sunk | while | flops 2449480704 | bytes 117054000 | solution.py:120
  183.2 2.2 dynamic-slice_convert_fusion.3
  188.1 2.1 broadcast_select_fusion.5
  190.9 1.5 copy.83
  194.3 1.5 multiply_convert_fusion.15
  204.2 2.2 dynamic-slice_convert_fusion.3
  209.4 1.8 copy-done.2
  211.3 1.5 copy.83
  214.7 1.5 multiply_convert_fusion.15
  224.6 2.2 dynamic-slice_convert_fusion.3
  229.8 1.8 copy-done.2
  235.1 1.5 multiply_convert_fusion.15
  244.9 2.2 dynamic-slice_convert_fusion.3
  250.2 1.8 copy-done.2
  252.0 1.5 copy.83
  255.4 1.6 multiply_convert_fusion.15
  265.3 2.2 dynamic-slice_convert_fusion.3
  270.5 1.8 copy-done.2
  275.8 1.6 multiply_convert_fusion.15
  285.7 2.2 dynamic-slice_convert_fusion.3
  290.9 1.8 copy-done.2
  296.1 1.5 multiply_convert_fusion.15
  306.0 2.2 dynamic-slice_convert_fusion.3
  311.3 1.8 copy-done.2
  316.5 1.5 multiply_convert_fusion.15
  326.4 2.2 dynamic-slice_convert_fusion.3
  331.6 1.8 copy-done.2
  336.9 1.5 multiply_convert_fusion.15
  344.8 20.5 %copy.53 = bf16[1,2048,1024]{2,0,1:T(2,128)(2,1)} copy(bf16[1,2048,1024]{1,2,0:T(8,128)(2,1)} %bitcast.89) | data formatting | bytes 8388608 | tf_op jit(solution)/shard_map/broadcast_in_dim | solution.py:121
  365.9 26.0 %reduce = bf16[2048,1024]{1,0:T(8,128)(2,1)} reduce(bf16[2048,1,1024]{2,1,0:T(2,128)(2,1)} %bitcast.87, bf16[]{:T(256)} %broadcast.105), dimensions={1}, to_apply=%bitcast.32.reduce_sub_computation | reduce | bytes 8388610
  391.8 7.8 %reshape.128 = bf16[8,2,131072]{2,1,0:T(2,128)(2,1)} reshape(bf16[2048,1024]{1,0:T(8,128)(2,1)} %reduce) | data formatting | bytes 8388608
  399.6 53.6 %all_to_all.53 = bf16[8,2,131072]{2,1,0:T(2,128)(2,1)} all-to-all(bf16[8,2,131072]{2,1,0:T(2,128)(2,1)} %reshape.128), channel_id=1, replica_groups=mesh['frame'=8,'head'=4] {'frame'}, dimensions={0} | all-to-all | bytes 8388608 | tf_op jit(solution)/shard_map/all_to_all | solution.py:121
  453.2 8.8 %reshape.129 = bf16[2048,1,1024]{2,1,0:T(2,128)(2,1)} reshape(bf16[8,2,131072]{2,1,0:T(2,128)(2,1)} %all_to_all.53) | data formatting | bytes 8388608
  462.0 5.1 copy.62
  467.2 17.2 %convolution_convert_fusion = bf16[1024,5120]{1,0:T(8,128)(2,1)} fusion(bf16[1024,1024]{1,0:T(8,128)(2,1)S(1)} %bitcast.91, bf16[1024,5120]{1,0:T(8,128)(2,1)} %param.21), kind=kOutput, calls=%fused_computation.36 | convolution fusion | flops 10742661120 | bytes 23068672 | tf_op jit(solution)/shard_map/dot_general | solution.py:124
  484.5 177.5 %reduce-scatter.2.cloned.1.call-done = bf16[1024,1280]{1,0:T(8,128)(2,1)} async-done(((bf16[1024,5120]{1,0:T(8,128)(2,1)}), bf16[1024,1280]{1,0:T(8,128)(2,1)}) %reduce-scatter.2.cloned.1.call-update) | async-done | bytes 2621456 | tf_op jit(solution)/shard_map/reduce_scatter | solution.py:125
  (259 shorter events, 114.7 us)
Async XLA Ops:
  6.5 127.6 %copy-start = (s32[4,8]{1,0:T(4,128)S(1)}, s32[4,8]{1,0:T(4,128)}, u32[]{:S(2)}) copy-start(s32[4,8]{1,0:T(4,128)} %param.17) | copy-start | bytes 388
  7.9 10.0 %all-to-all-start.2 = ((bf16[8,256,4]{1,2,0:T(4,128)(2,1)}), bf16[8,256,4]{1,2,0:T(4,128)(2,1)S(1)}, u32[]{:S(2)}, u32[]{:S(2)}) async-start(bf16[8,256,4]{1,2,0:T(4,128)(2,1)} %pad.13), calls=%async_computation.2 | async-start | bytes 32768 | tf_op jit(solution)/shard_map/all_to_all | solution.py:86
  17.1 5.3 copy-start.8
  17.8 53.7 %all-to-all-start.3 = ((bf16[8,256,1024]{2,1,0:T(8,128)(2,1)}), bf16[8,256,1024]{2,1,0:T(8,128)(2,1)}, u32[]{:S(2)}, u32[]{:S(2)}) async-start(bf16[8,256,1024]{2,1,0:T(8,128)(2,1)} %pad.14), calls=%async_computation.3 | async-start | bytes 8388608 | tf_op jit(solution)/shard_map/all_to_all | solution.py:83
  29.2 46.8 %copy-start.7 = (bf16[4,256,1024]{2,1,0:T(8,128)(2,1)S(1)}, bf16[4,256,1024]{2,1,0:T(8,128)(2,1)}, u32[]{:S(2)}) copy-start(bf16[4,256,1024]{2,1,0:T(8,128)(2,1)} %param.14) | copy-start | bytes 6291460
  71.5 53.7 %all-to-all-start = ((bf16[8,1,256,1024]{3,2,1,0:T(8,128)(2,1)}), bf16[8,1,256,1024]{3,2,1,0:T(8,128)(2,1)}, u32[]{:S(2)}, u32[]{:S(2)}) async-start(bf16[8,1,256,1024]{3,2,1,0:T(8,128)(2,1)} %broadcast_dynamic-update-slice_fusion.3), calls=%async_computation | async-start | bytes 8388608 | tf_op jit(solution)/shard_map/all_to_all | solution.py:72
  78.5 51.3 %copy-start.11 = (f32[1024]{0:T(1024)S(1)}, f32[1024]{0:T(1024)}, u32[]{:S(2)}) copy-start(f32[1024]{0:T(1024)} %param.20) | copy-start | bytes 12292
  78.5 51.3 %copy-start.5 = (bf16[4,512,256]{2,1,0:T(8,128)(2,1)S(1)}, bf16[4,512,256]{2,1,0:T(8,128)(2,1)}, u32[]{:S(2)}) copy-start(bf16[4,512,256]{2,1,0:T(8,128)(2,1)} %param.19) | copy-start | bytes 3145732
  125.1 53.7 %all-to-all-start.1 = ((bf16[8,256,1024]{2,1,0:T(8,128)(2,1)}), bf16[8,256,1024]{2,1,0:T(8,128)(2,1)}, u32[]{:S(2)}, u32[]{:S(2)}) async-start(bf16[8,256,1024]{2,1,0:T(8,128)(2,1)} %pad.12), calls=%async_computation.1 | async-start | bytes 8388608 | tf_op jit(solution)/shard_map/all_to_all | solution.py:85
  129.7 532.3 %reduce-scatter.2.cloned.1.call-start = ((), (), s32[]{:S(2)}) async-start(), calls=%async_computation.6 | async-start | bytes 13107200 | tf_op jit(solution)/shard_map/reduce_scatter | solution.py:125
  130.8 2.2 copy-start.3
  131.0 2.5 copy-start.12
  188.1 2.8 copy-start.2
  192.5 1.5 copy-start.6
  192.5 1.8 copy-start.9
  197.6 2.6 copy-start.10
  209.1 2.2 copy-start.2
  212.8 1.2 copy-start.4
  212.8 1.5 copy-start.6
  212.9 1.8 copy-start.9
  217.9 2.6 copy-start.10
  229.5 2.2 copy-start.2
  233.2 1.5 copy-start.6
  233.3 1.8 copy-start.9
  238.3 2.6 copy-start.10
  249.8 2.2 copy-start.2
  253.6 1.5 copy-start.6
  253.6 1.8 copy-start.9
  258.7 2.6 copy-start.10
  270.1 2.2 copy-start.2
  273.9 1.2 copy-start.4
  273.9 1.5 copy-start.6
  273.9 1.8 copy-start.9
  279.0 2.6 copy-start.10
  290.5 2.2 copy-start.2
  294.3 1.2 copy-start.4
  294.3 1.5 copy-start.6
  294.3 1.8 copy-start.9
  299.4 2.6 copy-start.10
  310.9 2.2 copy-start.2
  314.7 1.5 copy-start.6
  314.7 1.8 copy-start.9
  319.8 2.6 copy-start.10
  331.3 2.2 copy-start.2
  335.0 1.5 copy-start.6
  335.1 1.8 copy-start.9
  340.1 2.6 copy-start.10
  484.5 177.6 %copy-start.1 = (s32[4,8]{1,0:T(4,128)S(1)}, s32[4,8]{1,0:T(4,128)}, u32[]{:S(2)}) copy-start(s32[4,8]{1,0:T(4,128)} %param.17) | copy-start | bytes 388
  (5 other events, 6.1 us)
Sparse Core Ops, SparseCore 0:
  484.6 177.3 reduce-scatter.1
